TPU v7x, 32 devices: a whole 2x2x4 slice. The times are simulated.
32 devices in a mesh: grp: 4 (over y, core), frm: 8 (over z, x).
Axes of the slice: x: 2, y: 2, z: 4, core: 2. Of those that a mesh axis runs over, the one named last changes fastest.
Arguments:
- latents: bfloat16 [32, 512, 1152], P(('grp', 'frm')), may hold values from -6 to 6
- spatial_weight: bfloat16 [1152, 3456], replicated, may hold values from -1 to 1
- temporal_weight: bfloat16 [1152, 3456], replicated, may hold values from -1 to 1
- out_grad: bfloat16 [32, 512, 1152], P(('grp', 'frm')), may hold values from -6 to 6
Outputs:
- output: bfloat16 [32, 512, 1152], P(('grp', 'frm'))
- in_grad: bfloat16 [32, 512, 1152], P(('grp', 'frm'))
All inputs are finite; a program needn't handle non-finite values.
Results may differ from a plain program's by a relative error of at most 0.013.
Values may be sent and summed in bfloat16 or wider, within the bound.
A program may use at most 192 MiB of HBM per device.

v0:
```python
import functools
import math

import jax
import jax.numpy as jnp
from jax import lax
from jax.experimental import pallas as pl
from jax.experimental.pallas import tpu as pltpu
from jax.sharding import PartitionSpec as P

HEADS = 16
LANES = 128
WIN = 256
TILE = 384
F32 = jnp.float32
BF16 = jnp.bfloat16
LOG2E = math.log2(math.e)
VMEM_LIMIT = 60 * 1024 * 1024


def mm(a, b):
    return jnp.dot(a, b, preferred_element_type=F32)


def mm_bt(a, b):
    return lax.dot_general(a, b, (((1,), (1,)), ((), ())), preferred_element_type=F32)


def mm_at(a, b):
    return lax.dot_general(a, b, (((0,), (0,)), ((), ())), preferred_element_type=F32)


def window(head, head_dim, width):
    first = head * head_dim
    start = jnp.minimum(first // LANES, (width - WIN) // LANES) * LANES
    lane = lax.broadcasted_iota(jnp.int32, (1, WIN), 1) + start
    own = ((lane >= first) & (lane < first + head_dim)).astype(F32)
    return pl.multiple_of(start, LANES), own


def center_scale(tokens):
    values = tokens.astype(F32)
    center = values - jnp.mean(values, axis=-1, keepdims=True)
    spread = jnp.mean(center * center, axis=-1, keepdims=True)
    return center, lax.rsqrt(spread + 1e-06)


def norm_pull(tokens, cot):
    center, scale = center_scale(tokens)
    unit = center * scale
    return scale * (
        cot - jnp.mean(cot, axis=-1, keepdims=True) - unit * jnp.mean(cot * unit, axis=-1, keepdims=True)
    )


def project(rows_ref, weight_ref, mixed_ref):
    @pl.loop(0, weight_ref.shape[1] // TILE)
    def _(step):
        columns = pl.ds(pl.multiple_of(step * TILE, LANES), TILE)
        mixed_ref[:, columns] = mm(rows_ref[...], weight_ref[:, columns]).astype(BF16)


def project_pull(cots_ref, weight_ref, grad_ref):
    @pl.loop(0, weight_ref.shape[0] // TILE)
    def _(step):
        columns = pl.ds(pl.multiple_of(step * TILE, LANES), TILE)
        grad_ref[:, columns] = mm_bt(cots_ref[...], weight_ref[columns, :])


def spatial_kernel(x_ref, w_ref, hidden_ref, mixed_ref, expd_ref, out_ref, inv_ref, rows_ref):
    head = pl.program_id(0)
    tokens, width = x_ref.shape
    head_dim = width // HEADS
    rate = LOG2E / math.sqrt(head_dim)

    @pl.when(head == 0)
    def _():
        center, scale = center_scale(x_ref[...])
        rows_ref[...] = (center * scale).astype(BF16)
        project(rows_ref, w_ref, mixed_ref)
        out_ref[...] = jnp.zeros_like(out_ref)
        inv_ref[...] = jnp.zeros_like(inv_ref)

    start, own = window(head, head_dim, width)
    ownb = own.astype(BF16)
    cols = pl.ds(start, WIN)
    keys = mixed_ref[:, pl.ds(start + width, WIN)]
    values = mixed_ref[:, pl.ds(start + 2 * width, WIN)] * ownb + (1 - own).astype(BF16)
    block = tokens // 2
    for part in range(2):
        rows = slice(part * block, (part + 1) * block)
        query = mixed_ref[rows, cols] * ownb
        scores = mm_bt(query, keys)
        top = jnp.max(scores, axis=-1, keepdims=True)
        expd = jnp.exp2((scores - top) * rate).astype(BF16)
        expd_ref[0, rows, :] = expd
        mixout = mm(expd, values)
        total = jnp.max(mixout * (1 - own), axis=-1, keepdims=True)
        inv = own / total
        out_ref[rows, cols] += mixout * inv
        inv_ref[rows, cols] += inv

    @pl.when(head == HEADS - 1)
    def _():
        hidden_ref[...] = (x_ref[...].astype(F32) + out_ref[...]).astype(BF16)


def spatial_forward(x, w):
    tokens, width = x.shape
    full = lambda shape: pl.BlockSpec(shape, lambda h: (0, 0), pipeline_mode=pl.Buffered(1))
    return pl.pallas_call(
        spatial_kernel,
        grid=(HEADS,),
        in_specs=[full(x.shape), full(w.shape)],
        out_specs=[
            full(x.shape),
            full((tokens, 3 * width)),
            pl.BlockSpec((1, tokens, tokens), lambda h: (h, 0, 0)),
            full(x.shape),
            full(x.shape),
        ],
        out_shape=[
            jax.ShapeDtypeStruct(x.shape, BF16),
            jax.ShapeDtypeStruct((tokens, 3 * width), BF16),
            jax.ShapeDtypeStruct((HEADS, tokens, tokens), BF16),
            jax.ShapeDtypeStruct(x.shape, F32),
            jax.ShapeDtypeStruct(x.shape, F32),
        ],
        scratch_shapes=[pltpu.VMEM(x.shape, BF16)],
        compiler_params=pltpu.CompilerParams(vmem_limit_bytes=VMEM_LIMIT),
        cost_estimate=pl.CostEstimate(flops=8 * 10**9, bytes_accessed=30 * 10**6, transcendentals=4 * 10**6),
        name="spatial_fwd",
    )(x, w)


def spatial_pull_kernel(g_ref, x_ref, mixed_ref, out_ref, inv_ref, expd_ref, w_ref, grad_ref, acc_ref, cots_ref, rows_ref):
    head = pl.program_id(0)
    tokens, width = x_ref.shape
    head_dim = width // HEADS

    @pl.when(head == 0)
    def _():
        acc_ref[...] = jnp.zeros_like(acc_ref)

    start, own = window(head, head_dim, width)
    ownb = own.astype(BF16)
    cols = pl.ds(start, WIN)
    kcols = pl.ds(start + width, WIN)
    vcols = pl.ds(start + 2 * width, WIN)
    keys = mixed_ref[:, kcols]
    values = mixed_ref[:, vcols]
    block = tokens // 2
    dkeys = dvalues = None
    for part in range(2):
        rows = slice(part * block, (part + 1) * block)
        dmix = g_ref[rows, cols].astype(F32) * (inv_ref[rows, cols] * own)
        delta = jnp.sum(dmix * out_ref[rows, cols], axis=-1, keepdims=True)
        dmix = dmix.astype(BF16)
        expd = expd_ref[0, rows, :]
        dprobs = mm_bt(dmix, values)
        dscores = (expd.astype(F32) * (dprobs - delta)).astype(BF16)
        acc_ref[rows, cols] += mm(dscores, keys * ownb)
        dk = mm_at(dscores, mixed_ref[rows, cols] * ownb)
        dv = mm_at(expd, dmix)
        dkeys = dk if dkeys is None else dkeys + dk
        dvalues = dv if dvalues is None else dvalues + dv
    acc_ref[:, kcols] += dkeys
    acc_ref[:, vcols] += dvalues

    @pl.when(head == HEADS - 1)
    def _():
        scale = 1.0 / math.sqrt(head_dim)
        cots_ref[:, : 2 * width] = (acc_ref[:, : 2 * width] * scale).astype(BF16)
        cots_ref[:, 2 * width :] = acc_ref[:, 2 * width :].astype(BF16)
        project_pull(cots_ref, w_ref, rows_ref)
        grad_ref[...] = (g_ref[...].astype(F32) + norm_pull(x_ref[...], rows_ref[...])).astype(BF16)


def spatial_pull(g, x, mixed, out, inv, expd, w):
    tokens, width = x.shape
    full = lambda a: pl.BlockSpec(a.shape, lambda h: (0, 0), pipeline_mode=pl.Buffered(1))
    return pl.pallas_call(
        spatial_pull_kernel,
        grid=(HEADS,),
        in_specs=[full(g), full(x), full(mixed), full(out), full(inv),
                  pl.BlockSpec((1, tokens, tokens), lambda h: (h, 0, 0)), full(w)],
        out_specs=full(x),
        out_shape=jax.ShapeDtypeStruct(x.shape, BF16),
        scratch_shapes=[
            pltpu.VMEM((tokens, 3 * width), F32),
            pltpu.VMEM((tokens, 3 * width), BF16),
            pltpu.VMEM((tokens, width), F32),
        ],
        compiler_params=pltpu.CompilerParams(vmem_limit_bytes=VMEM_LIMIT),
        cost_estimate=pl.CostEstimate(flops=12 * 10**9, bytes_accessed=30 * 10**6, transcendentals=10**4),
        name="spatial_bwd",
    )(g, x, mixed, out, inv, expd, w)


def reorder(rows, inner, outer):
    row = lax.broadcasted_iota(jnp.int32, (rows, rows), 0)
    column = lax.broadcasted_iota(jnp.int32, (rows, rows), 1)
    return (column == (row % outer) * inner + row // outer).astype(F32).astype(BF16)


def temporal_kernel(frames, z_ref, g_ref, w_ref, res_ref, grad_ref, zt_ref, gt_ref, rows_ref, mixed_ref, out_ref, acc_ref, cots_ref):
    tokens, width = z_ref.shape
    head_dim = width // HEADS
    rate = LOG2E / math.sqrt(head_dim)
    patches = tokens // frames
    group = max(LANES, frames)

    order = reorder(tokens, patches, frames)
    zt_ref[...] = mm(order, z_ref[...]).astype(BF16)
    gt_ref[...] = mm(order, g_ref[...]).astype(BF16)
    center, scale = center_scale(zt_ref[...])
    rows_ref[...] = (center * scale).astype(BF16)
    project(rows_ref, w_ref, mixed_ref)
    out_ref[...] = jnp.zeros_like(out_ref)
    acc_ref[...] = jnp.zeros_like(acc_ref)
    same = (
        lax.broadcasted_iota(jnp.int32, (group, group), 0) // frames
        == lax.broadcasted_iota(jnp.int32, (group, group), 1) // frames
    )

    @pl.loop(0, HEADS)
    def _(head):
        start, own = window(head, head_dim, width)
        ownb = own.astype(BF16)
        cols = pl.ds(start, WIN)
        kcols = pl.ds(pl.multiple_of(start + width, LANES), WIN)
        vcols = pl.ds(pl.multiple_of(start + 2 * width, LANES), WIN)
        spans = [slice(part * group, (part + 1) * group) for part in range(tokens // group)]
        query = [mixed_ref[rows, cols] * ownb for rows in spans]
        keys = [mixed_ref[rows, kcols] * ownb for rows in spans]
        values = [mixed_ref[rows, vcols] * ownb for rows in spans]
        grads = [gt_ref[rows, cols].astype(F32) for rows in spans]
        scores = [jnp.where(same, mm_bt(q, k), -3e38) for q, k in zip(query, keys)]
        expd = [
            jnp.exp2((s - jnp.max(s, axis=-1, keepdims=True)) * rate).astype(BF16) for s in scores
        ]
        ones = (1 - own).astype(BF16)
        mixout = [mm(e, v + ones) for e, v in zip(expd, values)]
        inv = [own / jnp.max(m * (1 - own), axis=-1, keepdims=True) for m in mixout]
        mixout = [m * i for m, i in zip(mixout, inv)]
        dmix = [g * i for g, i in zip(grads, inv)]
        delta = [jnp.sum(d * m, axis=-1, keepdims=True) for d, m in zip(dmix, mixout)]
        dmix = [d.astype(BF16) for d in dmix]
        dscores = [
            (e.astype(F32) * (mm_bt(d, v) - t)).astype(BF16)
            for e, d, v, t in zip(expd, dmix, values, delta)
        ]
        dquery = [mm(s, k) for s, k in zip(dscores, keys)]
        dkeys = [mm_at(s, q) for s, q in zip(dscores, query)]
        dvalues = [mm_at(e, d) for e, d in zip(expd, dmix)]
        for rows, m, dq, dk, dv in zip(spans, mixout, dquery, dkeys, dvalues):
            out_ref[rows, cols] += m
            acc_ref[rows, cols] += dq
            acc_ref[rows, kcols] += dk
            acc_ref[rows, vcols] += dv

    scale = 1.0 / math.sqrt(head_dim)
    cots_ref[:, : 2 * width] = (acc_ref[:, : 2 * width] * scale).astype(BF16)
    cots_ref[:, 2 * width :] = acc_ref[:, 2 * width :].astype(BF16)
    rows_ref[...] = (zt_ref[...].astype(F32) + out_ref[...]).astype(BF16)
    project_pull(cots_ref, w_ref, out_ref)
    zt_ref[...] = (gt_ref[...].astype(F32) + norm_pull(zt_ref[...], out_ref[...])).astype(BF16)
    order = reorder(tokens, frames, patches)
    grad_ref[...] = mm(order, zt_ref[...]).astype(BF16)
    res_ref[...] = mm(order, rows_ref[...]).astype(BF16)


def temporal_both(z, g, w, frames):
    tokens, width = z.shape
    return pl.pallas_call(
        functools.partial(temporal_kernel, frames),
        out_shape=[jax.ShapeDtypeStruct(z.shape, BF16)] * 2,
        in_specs=[pl.BlockSpec(memory_space=pltpu.VMEM)] * 3,
        out_specs=[pl.BlockSpec(memory_space=pltpu.VMEM)] * 2,
        scratch_shapes=[
            pltpu.VMEM(z.shape, BF16),
            pltpu.VMEM(z.shape, BF16),
            pltpu.VMEM(z.shape, BF16),
            pltpu.VMEM((tokens, 3 * width), BF16),
            pltpu.VMEM(z.shape, F32),
            pltpu.VMEM((tokens, 3 * width), F32),
            pltpu.VMEM((tokens, 3 * width), BF16),
        ],
        compiler_params=pltpu.CompilerParams(vmem_limit_bytes=VMEM_LIMIT),
        cost_estimate=pl.CostEstimate(flops=12 * 10**9, bytes_accessed=15 * 10**6, transcendentals=10**6),
        name="temporal",
    )(z, g, w)


def swap(items):
    return lax.all_to_all(items, ("grp", "frm"), split_axis=0, concat_axis=0, tiled=True)


def local(frames, latents, spatial_weight, temporal_weight, out_grad):
    x = latents[0]
    grad_cols = swap(out_grad[0])
    hidden, mixed, expd, out, inv = spatial_forward(x, spatial_weight)
    hidden_cols = swap(hidden)
    result_cols, hidden_grad_cols = temporal_both(hidden_cols, grad_cols, temporal_weight, frames)
    hidden_grad = swap(hidden_grad_cols)
    output = swap(result_cols)
    in_grad = spatial_pull(hidden_grad, x, mixed, out, inv, expd, spatial_weight)
    return (output[None], in_grad[None])


def solution(mesh):
    frames = mesh.shape["grp"] * mesh.shape["frm"]
    return jax.shard_map(
        functools.partial(local, frames),
        mesh=mesh,
        in_specs=(P(("grp", "frm"), None, None), P(), P(), P(("grp", "frm"), None, None)),
        out_specs=(P(("grp", "frm"), None, None), P(("grp", "frm"), None, None)),
        check_vma=False,
    )
```

profile of v0, /device:TPU:0, one launch (start us, length us, event | category | flops | bytes accessed | tf_op | source)
XLA Modules:
  0.0 215.1 jit_solution(836404444623284608)
XLA Ops:
  0.6 7.3 %all-to-all-start.1 = ((bf16[32,16,1152]{2,1,0:T(8,128)(2,1)}), bf16[32,16,1152]{2,1,0:T(8,128)(2,1)S(1)}, u32[]{:S(2)}, u32[]{:S(2)}) async-start(bf16[32,16,1152]{2,1,0:T(8,128)(2,1)} %bitcast.11), calls=%async_computation.1 | async-start | bytes 2359296 | tf_op jit(solution)/shard_map/all_to_all | solution.py:296
  8.0 29.7 %spatial_fwd.1 = (bf16[512,1152]{1,0:T(8,128)(2,1)}, bf16[512,3456]{1,0:T(8,128)(2,1)}, bf16[16,512,512]{2,1,0:T(8,128)(2,1)}, f32[512,1152]{1,0:T(8,128)}, f32[512,1152]{1,0:T(8,128)}) custom-call(bf16[512,1152]{1,0:T(8,128)(2,1)} %bitcast.17, bf16[1152,3456]{1,0:T(8,128)(2,1)} %w_ref.5), custom_call_target="tpu_custom_call" | custom-call | flops 8000000000 | bytes 30000000 | tf_op jit(solution)/shard_map/spatial_fwd/pallas_call | solution.py:111
  37.7 0.6 all-to-all-done.1
  38.2 0.0 copy-start
  38.2 35.7 %all_to_all.42 = bf16[32,16,1152]{2,1,0:T(8,128)(2,1)} all-to-all(bf16[32,16,1152]{2,1,0:T(8,128)(2,1)} %bitcast.14), channel_id=1, replica_groups=mesh['grp'=4,'frm'=8] {'grp','frm'}, dimensions={0} | all-to-all | bytes 2359296 | tf_op jit(solution)/shard_map/all_to_all | solution.py:296
  73.9 0.0 copy-done
  73.9 41.4 %temporal.1 = (bf16[512,1152]{1,0:T(8,128)(2,1)}, bf16[512,1152]{1,0:T(8,128)(2,1)}) custom-call(bf16[512,1152]{1,0:T(8,128)(2,1)} %bitcast.15, bf16[512,1152]{1,0:T(8,128)(2,1)} %bitcast.12, bf16[1152,3456]{1,0:T(8,128)(2,1)} %w_ref.4), custom_call_target="tpu_custom_call" | custom-call | flops 12000000000 | bytes 15000000 | tf_op jit(solution)/shard_map/temporal/pallas_call | solution.py:275
  115.3 32.9 %all_to_all.43 = bf16[32,16,1152]{2,1,0:T(8,128)(2,1)S(1)} all-to-all(bf16[32,16,1152]{2,1,0:T(8,128)(2,1)} %bitcast.16), channel_id=1, replica_groups=mesh['grp'=4,'frm'=8] {'grp','frm'}, dimensions={0} | all-to-all | bytes 2359296 | tf_op jit(solution)/shard_map/all_to_all | solution.py:296
  148.3 2.8 %all-to-all-start.3 = ((bf16[32,16,1152]{2,1,0:T(8,128)(2,1)}), bf16[32,16,1152]{2,1,0:T(8,128)(2,1)S(1)}, u32[]{:S(2)}, u32[]{:S(2)}) async-start(bf16[32,16,1152]{2,1,0:T(8,128)(2,1)} %bitcast.7), calls=%async_computation.3 | async-start | bytes 2359296 | tf_op jit(solution)/shard_map/all_to_all | solution.py:296
  151.1 30.1 %all-to-all-done.3 = bf16[32,16,1152]{2,1,0:T(8,128)(2,1)S(1)} async-done(((bf16[32,16,1152]{2,1,0:T(8,128)(2,1)}), bf16[32,16,1152]{2,1,0:T(8,128)(2,1)S(1)}, u32[]{:S(2)}, u32[]{:S(2)}) %all-to-all-start.3) | async-done | bytes 1179680 | tf_op jit(solution)/shard_map/all_to_all | solution.py:296
  181.2 0.0 copy-start.1
  181.2 1.0 copy-done.1
  182.2 31.8 %spatial_bwd.1 = bf16[512,1152]{1,0:T(8,128)(2,1)} custom-call(bf16[512,1152]{1,0:T(8,128)(2,1)} %bitcast.13, bf16[512,1152]{1,0:T(8,128)(2,1)} %bitcast.18, bf16[512,3456]{1,0:T(8,128)(2,1)} %get-tuple-element.12.mixed_ref, f32[512,1152]{1,0:T(8,128)} %get-tuple-element.13.out_ref, f32[512,1152]{1,0:T(8,128)} %get-tuple-element.14.inv_ref, ...), custom_call_target="tpu_custom_call" | custom-call | flops 12000000000 | bytes 30000000 | tf_op jit(solution)/shard_map/spatial_bwd/pallas_call | solution.py:182
  214.1 1.0 copy.7
Async XLA Ops:
  0.6 37.6 %all-to-all-start.1 = ((bf16[32,16,1152]{2,1,0:T(8,128)(2,1)}), bf16[32,16,1152]{2,1,0:T(8,128)(2,1)S(1)}, u32[]{:S(2)}, u32[]{:S(2)}) async-start(bf16[32,16,1152]{2,1,0:T(8,128)(2,1)} %bitcast.11), calls=%async_computation.1 | async-start | bytes 2359296 | tf_op jit(solution)/shard_map/all_to_all | solution.py:296
  38.2 35.7 %copy-start = (bf16[32,16,1152]{2,1,0:T(8,128)(2,1)}, bf16[32,16,1152]{2,1,0:T(8,128)(2,1)S(1)}, u32[]{:S(2)}) copy-start(bf16[32,16,1152]{2,1,0:T(8,128)(2,1)S(1)} %all-to-all-done.1) | copy-start | bytes 3538948
  148.3 32.9 %all-to-all-start.3 = ((bf16[32,16,1152]{2,1,0:T(8,128)(2,1)}), bf16[32,16,1152]{2,1,0:T(8,128)(2,1)S(1)}, u32[]{:S(2)}, u32[]{:S(2)}) async-start(bf16[32,16,1152]{2,1,0:T(8,128)(2,1)} %bitcast.7), calls=%async_computation.3 | async-start | bytes 2359296 | tf_op jit(solution)/shard_map/all_to_all | solution.py:296
  181.2 1.0 copy-start.1
where the time goes:
time: 216 us; the launch traced here: 215 us
  Pallas kernels  103 us (48%)
  blocking collectives  68.6 us (32%)
  waiting for transfers between devices  30.7 us (14%)
  starting transfers between devices  10.2 us (5%)
    all_to_all x2, blocking collectives, swap(): lax.all_to_all(items, ('grp', 'frm'), split_axis=0, concat_axis=0, tiled=...  68.6 us
    pallas_call x1, Pallas kernels, temporal_both(): pl.pallas_call(functools.partial(temporal_kernel, frames), out_shape=[jax...  41.4 us
    pallas_call x1, Pallas kernels, spatial_pull(): pl.pallas_call(spatial_pull_kernel, grid=(HEADS,), in_specs=[full(g), ful...  31.8 us
    all_to_all x2, waiting for transfers between devices, swap(): lax.all_to_all(items, ('grp', 'frm'), split_axis=0, concat_axis=0, tiled=...  30.7 us
    pallas_call x1, Pallas kernels, spatial_forward(): pl.pallas_call(spatial_kernel, grid=(HEADS,), in_specs=[full(x.shape), fu...  29.7 us
    all_to_all x2, starting transfers between devices, swap(): lax.all_to_all(items, ('grp', 'frm'), split_axis=0, concat_axis=0, tiled=...  10.2 us
  transfers between devices with their start and end apart: 2, of which 2 were waited for; matrix products, arithmetic and copies ran while one was open for 0% of the time, Pallas kernels for 14%

commit v1 on v0

--- a/solution.py
+++ b/solution.py
@@ -8,10 +8,13 @@
 from jax.experimental.pallas import tpu as pltpu
 from jax.sharding import PartitionSpec as P
 
+
 HEADS = 16
 LANES = 128
 WIN = 256
 TILE = 384
+CHUNKS = 2
+CHAINS = 8
 F32 = jnp.float32
 BF16 = jnp.bfloat16
 LOG2E = math.log2(math.e)
@@ -67,7 +70,8 @@
         grad_ref[:, columns] = mm_bt(cots_ref[...], weight_ref[columns, :])
 
 
-def spatial_kernel(x_ref, w_ref, hidden_ref, mixed_ref, expd_ref, out_ref, inv_ref, rows_ref):
+def spatial_kernel(x_ref, w_ref, *refs):
+    hidden_refs, (mixed_ref, expd_ref, out_ref, inv_ref, rows_ref) = refs[:CHUNKS], refs[CHUNKS:]
     head = pl.program_id(0)
     tokens, width = x_ref.shape
     head_dim = width // HEADS
@@ -86,23 +90,23 @@
     cols = pl.ds(start, WIN)
     keys = mixed_ref[:, pl.ds(start + width, WIN)]
     values = mixed_ref[:, pl.ds(start + 2 * width, WIN)] * ownb + (1 - own).astype(BF16)
-    block = tokens // 2
-    for part in range(2):
-        rows = slice(part * block, (part + 1) * block)
-        query = mixed_ref[rows, cols] * ownb
-        scores = mm_bt(query, keys)
-        top = jnp.max(scores, axis=-1, keepdims=True)
-        expd = jnp.exp2((scores - top) * rate).astype(BF16)
-        expd_ref[0, rows, :] = expd
-        mixout = mm(expd, values)
-        total = jnp.max(mixout * (1 - own), axis=-1, keepdims=True)
-        inv = own / total
-        out_ref[rows, cols] += mixout * inv
-        inv_ref[rows, cols] += inv
+    block = tokens // CHUNKS
+    half = tokens // 2
+    spans = [slice(0, half), slice(half, tokens)]
+    scores = [mm_bt(mixed_ref[rows, cols] * ownb, keys) for rows in spans]
+    expd = [jnp.exp2((s - jnp.max(s, axis=-1, keepdims=True)) * rate).astype(BF16) for s in scores]
+    mixout = [mm(e, values) for e in expd]
+    inv = [own / jnp.max(m * (1 - own), axis=-1, keepdims=True) for m in mixout]
+    for rows, e, m, i in zip(spans, expd, mixout, inv):
+        expd_ref[0, rows, :] = e
+        out_ref[rows, cols] += m * i
+        inv_ref[rows, cols] += i
 
     @pl.when(head == HEADS - 1)
     def _():
-        hidden_ref[...] = (x_ref[...].astype(F32) + out_ref[...]).astype(BF16)
+        for part, hidden_ref in enumerate(hidden_refs):
+            rows = slice(part * block, (part + 1) * block)
+            hidden_ref[...] = (x_ref[rows, :].astype(F32) + out_ref[rows, :]).astype(BF16)
 
 
 def spatial_forward(x, w):
@@ -112,15 +116,13 @@
         spatial_kernel,
         grid=(HEADS,),
         in_specs=[full(x.shape), full(w.shape)],
-        out_specs=[
-            full(x.shape),
+        out_specs=[full((tokens // CHUNKS, width))] * CHUNKS + [
             full((tokens, 3 * width)),
             pl.BlockSpec((1, tokens, tokens), lambda h: (h, 0, 0)),
             full(x.shape),
             full(x.shape),
         ],
-        out_shape=[
-            jax.ShapeDtypeStruct(x.shape, BF16),
+        out_shape=[jax.ShapeDtypeStruct((tokens // CHUNKS, width), BF16)] * CHUNKS + [
             jax.ShapeDtypeStruct((tokens, 3 * width), BF16),
             jax.ShapeDtypeStruct((HEADS, tokens, tokens), BF16),
             jax.ShapeDtypeStruct(x.shape, F32),
@@ -133,7 +135,9 @@
     )(x, w)
 
 
-def spatial_pull_kernel(g_ref, x_ref, mixed_ref, out_ref, inv_ref, expd_ref, w_ref, grad_ref, acc_ref, cots_ref, rows_ref):
+def spatial_pull_kernel(*refs):
+    g_refs = refs[:CHUNKS]
+    (x_ref, mixed_ref, out_ref, inv_ref, expd_ref, w_ref, grad_ref, acc_ref, cots_ref, rows_ref) = refs[CHUNKS:]
     head = pl.program_id(0)
     tokens, width = x_ref.shape
     head_dim = width // HEADS
@@ -149,11 +153,11 @@
     vcols = pl.ds(start + 2 * width, WIN)
     keys = mixed_ref[:, kcols]
     values = mixed_ref[:, vcols]
-    block = tokens // 2
+    block = tokens // CHUNKS
     dkeys = dvalues = None
-    for part in range(2):
+    for part in range(CHUNKS):
         rows = slice(part * block, (part + 1) * block)
-        dmix = g_ref[rows, cols].astype(F32) * (inv_ref[rows, cols] * own)
+        dmix = g_refs[part][:, cols].astype(F32) * (inv_ref[rows, cols] * own)
         delta = jnp.sum(dmix * out_ref[rows, cols], axis=-1, keepdims=True)
         dmix = dmix.astype(BF16)
         expd = expd_ref[0, rows, :]
@@ -173,16 +177,19 @@
         cots_ref[:, : 2 * width] = (acc_ref[:, : 2 * width] * scale).astype(BF16)
         cots_ref[:, 2 * width :] = acc_ref[:, 2 * width :].astype(BF16)
         project_pull(cots_ref, w_ref, rows_ref)
-        grad_ref[...] = (g_ref[...].astype(F32) + norm_pull(x_ref[...], rows_ref[...])).astype(BF16)
-
-
-def spatial_pull(g, x, mixed, out, inv, expd, w):
+        for part, g_ref in enumerate(g_refs):
+            rows = slice(part * block, (part + 1) * block)
+            pulled = norm_pull(x_ref[rows, :], rows_ref[rows, :])
+            grad_ref[rows, :] = (g_ref[...].astype(F32) + pulled).astype(BF16)
+
+
+def spatial_pull(grads, x, mixed, out, inv, expd, w):
     tokens, width = x.shape
     full = lambda a: pl.BlockSpec(a.shape, lambda h: (0, 0), pipeline_mode=pl.Buffered(1))
     return pl.pallas_call(
         spatial_pull_kernel,
         grid=(HEADS,),
-        in_specs=[full(g), full(x), full(mixed), full(out), full(inv),
+        in_specs=[full(g) for g in grads] + [full(x), full(mixed), full(out), full(inv),
                   pl.BlockSpec((1, tokens, tokens), lambda h: (h, 0, 0)), full(w)],
         out_specs=full(x),
         out_shape=jax.ShapeDtypeStruct(x.shape, BF16),
@@ -194,7 +201,7 @@
         compiler_params=pltpu.CompilerParams(vmem_limit_bytes=VMEM_LIMIT),
         cost_estimate=pl.CostEstimate(flops=12 * 10**9, bytes_accessed=30 * 10**6, transcendentals=10**4),
         name="spatial_bwd",
-    )(g, x, mixed, out, inv, expd, w)
+    )(*grads, x, mixed, out, inv, expd, w)
 
 
 def reorder(rows, inner, outer):
@@ -223,25 +230,29 @@
         == lax.broadcasted_iota(jnp.int32, (group, group), 1) // frames
     )
 
-    @pl.loop(0, HEADS)
-    def _(head):
-        start, own = window(head, head_dim, width)
-        ownb = own.astype(BF16)
-        cols = pl.ds(start, WIN)
-        kcols = pl.ds(pl.multiple_of(start + width, LANES), WIN)
-        vcols = pl.ds(pl.multiple_of(start + 2 * width, LANES), WIN)
-        spans = [slice(part * group, (part + 1) * group) for part in range(tokens // group)]
-        query = [mixed_ref[rows, cols] * ownb for rows in spans]
-        keys = [mixed_ref[rows, kcols] * ownb for rows in spans]
-        values = [mixed_ref[rows, vcols] * ownb for rows in spans]
-        grads = [gt_ref[rows, cols].astype(F32) for rows in spans]
+    spans = [slice(part * group, (part + 1) * group) for part in range(tokens // group)]
+    batch = min(HEADS, max(1, CHAINS // len(spans)))
+
+    @pl.loop(0, HEADS // batch)
+    def _(step):
+        sites = []
+        for offset in range(batch):
+            start, own = window(step * batch + offset, head_dim, width)
+            cols = pl.ds(start, WIN)
+            kcols = pl.ds(pl.multiple_of(start + width, LANES), WIN)
+            vcols = pl.ds(pl.multiple_of(start + 2 * width, LANES), WIN)
+            sites += [(rows, cols, kcols, vcols, own) for rows in spans]
+        owns = [site[4] for site in sites]
+        query = [mixed_ref[r, c] * o.astype(BF16) for r, c, _, _, o in sites]
+        keys = [mixed_ref[r, c] * o.astype(BF16) for r, _, c, _, o in sites]
+        values = [mixed_ref[r, c] * o.astype(BF16) for r, _, _, c, o in sites]
+        grads = [gt_ref[r, c].astype(F32) for r, c, _, _, _ in sites]
         scores = [jnp.where(same, mm_bt(q, k), -3e38) for q, k in zip(query, keys)]
         expd = [
             jnp.exp2((s - jnp.max(s, axis=-1, keepdims=True)) * rate).astype(BF16) for s in scores
         ]
-        ones = (1 - own).astype(BF16)
-        mixout = [mm(e, v + ones) for e, v in zip(expd, values)]
-        inv = [own / jnp.max(m * (1 - own), axis=-1, keepdims=True) for m in mixout]
+        mixout = [mm(e, v + (1 - o).astype(BF16)) for e, v, o in zip(expd, values, owns)]
+        inv = [o / jnp.max(m * (1 - o), axis=-1, keepdims=True) for m, o in zip(mixout, owns)]
         mixout = [m * i for m, i in zip(mixout, inv)]
         dmix = [g * i for g, i in zip(grads, inv)]
         delta = [jnp.sum(d * m, axis=-1, keepdims=True) for d, m in zip(dmix, mixout)]
@@ -253,11 +264,11 @@
         dquery = [mm(s, k) for s, k in zip(dscores, keys)]
         dkeys = [mm_at(s, q) for s, q in zip(dscores, query)]
         dvalues = [mm_at(e, d) for e, d in zip(expd, dmix)]
-        for rows, m, dq, dk, dv in zip(spans, mixout, dquery, dkeys, dvalues):
-            out_ref[rows, cols] += m
-            acc_ref[rows, cols] += dq
-            acc_ref[rows, kcols] += dk
-            acc_ref[rows, vcols] += dv
+        for (r, c, kc, vc, _), m, dq, dk, dv in zip(sites, mixout, dquery, dkeys, dvalues):
+            out_ref[r, c] += m
+            acc_ref[r, c] += dq
+            acc_ref[r, kc] += dk
+            acc_ref[r, vc] += dv
 
     scale = 1.0 / math.sqrt(head_dim)
     cots_ref[:, : 2 * width] = (acc_ref[:, : 2 * width] * scale).astype(BF16)
@@ -292,26 +303,39 @@
     )(z, g, w)
 
 
-def swap(items):
-    return lax.all_to_all(items, ("grp", "frm"), split_axis=0, concat_axis=0, tiled=True)
+def swap(items, axis=0):
+    return lax.all_to_all(items, ("grp", "frm"), split_axis=axis, concat_axis=axis, tiled=True)
 
 
 def local(frames, latents, spatial_weight, temporal_weight, out_grad):
-    x = latents[0]
-    grad_cols = swap(out_grad[0])
-    hidden, mixed, expd, out, inv = spatial_forward(x, spatial_weight)
-    hidden_cols = swap(hidden)
-    result_cols, hidden_grad_cols = temporal_both(hidden_cols, grad_cols, temporal_weight, frames)
-    hidden_grad = swap(hidden_grad_cols)
-    output = swap(result_cols)
-    in_grad = spatial_pull(hidden_grad, x, mixed, out, inv, expd, spatial_weight)
+    x, grad = latents[0], out_grad[0]
+    tokens, width = x.shape
+    shape = (CHUNKS, frames, tokens // (CHUNKS * frames), width)
+    grad_cols = swap(grad.reshape(shape), 1)
+    grad_cols = grad_cols.reshape(CHUNKS, tokens // CHUNKS, width)
+    *hidden, mixed, expd, out, inv = spatial_forward(x, spatial_weight)
+    hidden_cols = [swap(piece) for piece in hidden]
+    results, hidden_grads = [], []
+    for part, piece in enumerate(hidden_cols):
+        result, pulled = temporal_both(piece, grad_cols[part], temporal_weight, frames)
+        results.append(result)
+        hidden_grads.append(swap(pulled))
+    results, hidden_grads = lax.optimization_barrier((results, hidden_grads))
+    stacked = jnp.stack(results).reshape(shape)
+    output = swap(stacked, 1)
+    output = output.reshape(tokens, width)
+    in_grad = spatial_pull(hidden_grads, x, mixed, out, inv, expd, spatial_weight)
     return (output[None], in_grad[None])
 
 
 def solution(mesh):
     frames = mesh.shape["grp"] * mesh.shape["frm"]
+
+    def body(*args):
+        return local(frames, *args)
+
     return jax.shard_map(
-        functools.partial(local, frames),
+        body,
         mesh=mesh,
         in_specs=(P(("grp", "frm"), None, None), P(), P(), P(("grp", "frm"), None, None)),
         out_specs=(P(("grp", "frm"), None, None), P(("grp", "frm"), None, None)),

time: 216 us -> 201 us (0.931)
  waiting for transfers between devices: 30.7 us -> 17.5 us
  blocking collectives: 68.6 us -> 55.9 us
  starting transfers between devices: 10.2 us -> 18.6 us
    all_to_all x2 -> x4, waiting for transfers between devices: 30.7 us -> 17.5 us  [swap(): lax.all_to_all(items, ('grp', 'frm'), split_axis=axis, concat_axis=axis,...]
    all_to_all x2, blocking collectives: 68.6 us -> 55.9 us  [swap(): lax.all_to_all(items, ('grp', 'frm'), split_axis=axis, concat_axis=axis,...]
    all_to_all x2 -> x4, starting transfers between devices: 10.2 us -> 18.6 us  [swap(): lax.all_to_all(items, ('grp', 'frm'), split_axis=axis, concat_axis=axis,...]
    pallas_call x1 -> x2, Pallas kernels: 41.4 us -> 42.6 us  [temporal_both(): pl.pallas_call(functools.partial(temporal_kernel, frames), out_shape=[jax...]
  transfers between devices with their start and end apart: 2 -> 4, of which waited for: 2 -> 1; matrix products, arithmetic and copies ran while one was open for 0% -> 1% of each run, Pallas kernels for 14% -> 37%
where the time goes in v1:
time: 201 us; the launch traced here: 200 us
  Pallas kernels  104 us (52%)
  blocking collectives  55.9 us (28%)
  starting transfers between devices  18.6 us (9%)
  waiting for transfers between devices  17.5 us (9%)
  local copies, waits for them, and re-layouts  2.33 us (1%)
    all_to_all x2, blocking collectives, swap(): lax.all_to_all(items, ('grp', 'frm'), split_axis=axis, concat_axis=axis,...  55.9 us
    pallas_call x2, Pallas kernels, temporal_both(): pl.pallas_call(functools.partial(temporal_kernel, frames), out_shape=[jax...  42.6 us
    pallas_call x1, Pallas kernels, spatial_pull(): pl.pallas_call(spatial_pull_kernel, grid=(HEADS,), in_specs=[full(g) for...  31.9 us
    pallas_call x1, Pallas kernels, spatial_forward(): pl.pallas_call(spatial_kernel, grid=(HEADS,), in_specs=[full(x.shape), fu...  29.6 us
    all_to_all x4, starting transfers between devices, swap(): lax.all_to_all(items, ('grp', 'frm'), split_axis=axis, concat_axis=axis,...  18.6 us
    all_to_all x4, waiting for transfers between devices, swap(): lax.all_to_all(items, ('grp', 'frm'), split_axis=axis, concat_axis=axis,...  17.5 us
  transfers between devices with their start and end apart: 4, of which 1 were waited for; matrix products, arithmetic and copies ran while one was open for 1% of the time, Pallas kernels for 37%

profile of v1, /device:TPU:0, one launch (start us, length us, event | category | flops | bytes accessed | tf_op | source)
XLA Modules:
  0.0 200.2 jit_solution(11514367643546956374)
XLA Ops:
  0.6 29.6 %spatial_fwd.1 = (bf16[256,1152]{1,0:T(8,128)(2,1)}, bf16[256,1152]{1,0:T(8,128)(2,1)}, bf16[512,3456]{1,0:T(8,128)(2,1)}, bf16[16,512,512]{2,1,0:T(8,128)(2,1)}...) custom-call(bf16[512,1152]{1,0:T(8,128)(2,1)} %bitcast.33, bf16[1152,3456]{1,0:T(8,128)(2,1)} %refs_7_.1), custom_call_target="tpu_custom_call" | custom-call | flops 8000000000 | bytes 30000000 | tf_op jit(solution)/shard_map/spatial_fwd/pallas_call | solution.py:115
  30.2 7.3 %all-to-all-start.2 = ((bf16[32,8,1152]{2,1,0:T(8,128)(2,1)}), bf16[32,8,1152]{2,1,0:T(8,128)(2,1)S(1)}, u32[]{:S(2)}, u32[]{:S(2)}) async-start(bf16[32,8,1152]{2,1,0:T(8,128)(2,1)} %bitcast.29), calls=%async_computation.2 | async-start | bytes 1179648 | tf_op jit(solution)/shard_map/all_to_all | solution.py:307
  37.5 0.0 copy-done
  37.6 0.1 copy.8
  37.7 17.5 %all-to-all-done.2 = bf16[32,8,1152]{2,1,0:T(8,128)(2,1)S(1)} async-done(((bf16[32,8,1152]{2,1,0:T(8,128)(2,1)}), bf16[32,8,1152]{2,1,0:T(8,128)(2,1)S(1)}, u32[]{:S(2)}, u32[]{:S(2)}) %all-to-all-start.2) | async-done | bytes 589856 | tf_op jit(solution)/shard_map/all_to_all | solution.py:307
  55.2 32.4 %all_to_all.56 = bf16[2,32,8,1152]{3,2,0,1:T(8,128)(2,1)S(1)} all-to-all(bf16[2,32,8,1152]{3,2,0,1:T(8,128)(2,1)S(1)} %copy.8), channel_id=1, replica_groups=mesh['grp'=4,'frm'=8] {'grp','frm'}, dimensions={1} | all-to-all | bytes 2359296 | tf_op jit(solution)/shard_map/all_to_all | solution.py:307
  87.6 0.0 copy-done.3
  87.6 2.6 %all-to-all-start = ((bf16[32,8,1152]{2,1,0:T(8,128)(2,1)}), bf16[32,8,1152]{2,1,0:T(8,128)(2,1)S(1)}, u32[]{:S(2)}, u32[]{:S(2)}) async-start(bf16[32,8,1152]{2,1,0:T(8,128)(2,1)} %bitcast.1), calls=%async_computation | async-start | bytes 1179648 | tf_op jit(solution)/shard_map/all_to_all | solution.py:307
  90.2 1.1 slice_bitcast_fusion
  91.3 21.3 %temporal.3 = (bf16[256,1152]{1,0:T(8,128)(2,1)}, bf16[256,1152]{1,0:T(8,128)(2,1)}) custom-call(bf16[256,1152]{1,0:T(8,128)(2,1)} %bitcast.26, bf16[256,1152]{1,0:T(8,128)(2,1)} %get-tuple-element.30.g_ref, bf16[1152,3456]{1,0:T(8,128)(2,1)} %w_ref.5), custom_call_target="tpu_custom_call" | custom-call | flops 12000000000 | bytes 15000000 | tf_op jit(solution)/shard_map/temporal/pallas_call | solution.py:286
  112.6 0.0 all-to-all-done
  112.6 6.0 %all-to-all-start.4 = ((bf16[32,8,1152]{2,1,0:T(8,128)(2,1)}), bf16[32,8,1152]{2,1,0:T(8,128)(2,1)S(1)}, u32[]{:S(2)}, u32[]{:S(2)}) async-start(bf16[32,8,1152]{2,1,0:T(8,128)(2,1)} %bitcast.27), calls=%async_computation.4 | async-start | bytes 1179648 | tf_op jit(solution)/shard_map/all_to_all | solution.py:307
  118.7 0.0 copy-done.2
  118.7 21.3 %temporal.2 = (bf16[256,1152]{1,0:T(8,128)(2,1)}, bf16[256,1152]{1,0:T(8,128)(2,1)}) custom-call(bf16[256,1152]{1,0:T(8,128)(2,1)} %bitcast.25, bf16[256,1152]{1,0:T(8,128)(2,1)} %get-tuple-element.31.g_ref, bf16[1152,3456]{1,0:T(8,128)(2,1)} %w_ref.5), custom_call_target="tpu_custom_call" | custom-call | flops 12000000000 | bytes 15000000 | tf_op jit(solution)/shard_map/temporal/pallas_call | solution.py:286
  140.0 0.0 all-to-all-done.4
  140.0 0.0 copy-start.1
  140.0 23.4 %all_to_all.57 = bf16[32,8,1152]{2,1,0:T(8,128)(2,1)} all-to-all(bf16[32,8,1152]{2,1,0:T(8,128)(2,1)} %bitcast.30), channel_id=1, replica_groups=mesh['grp'=4,'frm'=8] {'grp','frm'}, dimensions={0} | all-to-all | bytes 1179648 | tf_op jit(solution)/shard_map/all_to_all | solution.py:307
  163.4 0.0 copy-done.4
  163.4 0.0 copy-done.5
  163.4 1.1 pad_maximum_fusion
  164.5 2.7 %all-to-all-start.5 = ((bf16[2,32,8,1152]{3,2,0,1:T(8,128)(2,1)}), bf16[2,32,8,1152]{3,2,0,1:T(8,128)(2,1)S(1)}, u32[]{:S(2)}, u32[]{:S(2)}) async-start(bf16[2,32,8,1152]{3,2,0,1:T(8,128)(2,1)} %pad_maximum_fusion), calls=%async_computation.5 | async-start | bytes 2359296 | tf_op jit(solution)/shard_map/all_to_all | solution.py:307
  167.2 31.9 %spatial_bwd.1 = bf16[512,1152]{1,0:T(8,128)(2,1)} custom-call(bf16[256,1152]{1,0:T(8,128)(2,1)} %bitcast.28, bf16[256,1152]{1,0:T(8,128)(2,1)} %bitcast.24, bf16[512,1152]{1,0:T(8,128)(2,1)} %bitcast.34, bf16[512,3456]{1,0:T(8,128)(2,1)} %get-tuple-element.26.refs_3_, f32[512,1152]{1,0:T(8,128)} %get-tuple-element.27.refs_4_, ...), custom_call_target="tpu_custom_call" | custom-call | flops 12000000000 | bytes 30000000 | tf_op jit(solution)/shard_map/spatial_bwd/pallas_call | solution.py:189
  199.1 0.0 all-to-all-done.5
  199.1 1.1 copy.11
  (6 shorter events, 0.0 us)
Async XLA Ops:
  30.2 7.3 %copy-start = (bf16[1,512,1152]{2,1,0:T(8,128)(2,1)S(1)}, bf16[1,512,1152]{2,1,0:T(8,128)(2,1)}, u32[]{:S(2)}) copy-start(bf16[1,512,1152]{2,1,0:T(8,128)(2,1)} %param.7) | copy-start | bytes 3538948
  30.2 25.0 %all-to-all-start.2 = ((bf16[32,8,1152]{2,1,0:T(8,128)(2,1)}), bf16[32,8,1152]{2,1,0:T(8,128)(2,1)S(1)}, u32[]{:S(2)}, u32[]{:S(2)}) async-start(bf16[32,8,1152]{2,1,0:T(8,128)(2,1)} %bitcast.29), calls=%async_computation.2 | async-start | bytes 1179648 | tf_op jit(solution)/shard_map/all_to_all | solution.py:307
  55.2 32.4 %copy-start.3 = (bf16[32,8,1152]{2,1,0:T(8,128)(2,1)}, bf16[32,8,1152]{2,1,0:T(8,128)(2,1)S(1)}, u32[]{:S(2)}) copy-start(bf16[32,8,1152]{2,1,0:T(8,128)(2,1)S(1)} %all-to-all-done.2) | copy-start | bytes 1769476
  87.6 25.0 %all-to-all-start = ((bf16[32,8,1152]{2,1,0:T(8,128)(2,1)}), bf16[32,8,1152]{2,1,0:T(8,128)(2,1)S(1)}, u32[]{:S(2)}, u32[]{:S(2)}) async-start(bf16[32,8,1152]{2,1,0:T(8,128)(2,1)} %bitcast.1), calls=%async_computation | async-start | bytes 1179648 | tf_op jit(solution)/shard_map/all_to_all | solution.py:307
  112.6 6.0 %copy-start.2 = (bf16[32,8,1152]{2,1,0:T(8,128)(2,1)}, bf16[32,8,1152]{2,1,0:T(8,128)(2,1)S(1)}, u32[]{:S(2)}) copy-start(bf16[32,8,1152]{2,1,0:T(8,128)(2,1)S(1)} %all-to-all-done) | copy-start | bytes 1769476
  112.6 27.3 %all-to-all-start.4 = ((bf16[32,8,1152]{2,1,0:T(8,128)(2,1)}), bf16[32,8,1152]{2,1,0:T(8,128)(2,1)S(1)}, u32[]{:S(2)}, u32[]{:S(2)}) async-start(bf16[32,8,1152]{2,1,0:T(8,128)(2,1)} %bitcast.27), calls=%async_computation.4 | async-start | bytes 1179648 | tf_op jit(solution)/shard_map/all_to_all | solution.py:307
  139.9 23.4 %copy-start.4 = (bf16[256,1152]{1,0:T(8,128)(2,1)S(1)}, bf16[256,1152]{1,0:T(8,128)(2,1)}, u32[]{:S(2)}) copy-start(bf16[256,1152]{1,0:T(8,128)(2,1)} %get-tuple-element.23) | copy-start | bytes 1769476
  140.0 23.4 %copy-start.5 = (bf16[256,1152]{1,0:T(8,128)(2,1)S(1)}, bf16[256,1152]{1,0:T(8,128)(2,1)}, u32[]{:S(2)}) copy-start(bf16[256,1152]{1,0:T(8,128)(2,1)} %get-tuple-element.22) | copy-start | bytes 1769476
  140.0 24.6 %copy-start.1 = (bf16[32,8,1152]{2,1,0:T(8,128)(2,1)}, bf16[32,8,1152]{2,1,0:T(8,128)(2,1)S(1)}, u32[]{:S(2)}) copy-start(bf16[32,8,1152]{2,1,0:T(8,128)(2,1)S(1)} %all-to-all-done.4) | copy-start | bytes 1769476
  164.5 34.6 %all-to-all-start.5 = ((bf16[2,32,8,1152]{3,2,0,1:T(8,128)(2,1)}), bf16[2,32,8,1152]{3,2,0,1:T(8,128)(2,1)S(1)}, u32[]{:S(2)}, u32[]{:S(2)}) async-start(bf16[2,32,8,1152]{3,2,0,1:T(8,128)(2,1)} %pad_maximum_fusion), calls=%async_computation.5 | async-start | bytes 2359296 | tf_op jit(solution)/shard_map/all_to_all | solution.py:307
